TPU v7x, 256 devices: a whole 4x4x8 slice. The times are simulated.
256 devices in a mesh: store: 32 (over y, z), tp: 8 (over x, core).
Axes of the slice: x: 4, y: 4, z: 8, core: 2. Of those that a mesh axis runs over, the one named last changes fastest.
Arguments:
- queries: bfloat16 [32768, 8192], P('store', 'tp')
- fresh_kv: bfloat16 [2, 32768, 1024], P(None, ('store', 'tp'))
- page_pool: bfloat16 [2048, 2, 128, 1024], P('store', None, None, 'tp')
- page_host: int32 [128, 8], P('store'), may hold values from 0 to 31, as said below
- page_slot: int32 [128, 8], P('store'), may hold values from 0 to 63, as said below
- prefix_len: int32 [128], P('store'), may hold values from 513 to 1024
- fresh_len: int32 [32, 4], P('store'), may hold values from 1 to 384, 1024 in all within a row
Outputs:
- attention: bfloat16 [32768, 8192], P('store', 'tp')
Inputs may be any that keep to these rules, and one draw needn't show every extreme that they name: `page_host`: page p of request r is read only if p < ceil(prefix_len[r] / 128). Among the pages read by the 4 requests of one host, at most 2 lie on any one host; in every draw some host holds exactly 2 of the pages read by each host. `page_slot`: several entries may name the same stored page. `fresh_len`: the requests of a host own consecutive rows of its block, in order.
All inputs are finite; a program needn't handle non-finite values.
Results may differ from a plain program's by a relative error of at most 0.0041.
Values may be sent and summed in bfloat16 or wider, within the bound.
A program may use at most 128 MiB of HBM per device.

v0:
```python
import math
import jax
import jax.numpy as jnp
from jax import lax
from jax.sharding import PartitionSpec as P

HD = 128
REQ_HOST = 4
PAGE = 128
PAGES_MAX = 8
MOST_NEW = 384


def plan_requests(owners, slot_ids, prefix, stores, capacity):
    entry_count = owners.shape[0] * owners.shape[1]
    page_count = (prefix + PAGE - 1) // PAGE
    in_use = (jnp.arange(owners.shape[1], dtype=jnp.int32)[None, :] < page_count[:, None]).reshape(
        entry_count
    )
    flat_owners = owners.reshape(entry_count)
    flat_slots = slot_ids.reshape(entry_count)
    entries = jnp.arange(entry_count, dtype=jnp.int32)
    same_owner = (
        (flat_owners[:, None] == flat_owners[None, :])
        & in_use[None, :]
        & (entries[None, :] < entries[:, None])
    )
    owner_rank = jnp.sum(same_owner.astype(jnp.int32), axis=1)
    position = jnp.where(in_use, flat_owners * capacity + owner_rank, 0)
    target = jnp.arange(stores * capacity, dtype=jnp.int32)
    matches = (position[:, None] == target[None, :]) & in_use[:, None]
    buffer = jnp.sum(jnp.where(matches, flat_slots[:, None], 0), axis=0)
    return (buffer.reshape(stores, capacity), position)


def attend(q_rows, key_rows, value_rows, key_valid):
    scores = jnp.einsum("mkgd,nkd->kgmn", q_rows, key_rows, preferred_element_type=jnp.float32) * (
        1.0 / math.sqrt(HD)
    )
    row_top = jnp.max(jnp.where(key_valid, scores, -1e30), axis=-1, keepdims=True)
    weights = jnp.where(key_valid, jnp.exp(scores - row_top), 0.0)
    row_total = jnp.sum(weights, axis=-1)
    rounded = weights.astype(jnp.bfloat16)
    mixed_rows = jnp.einsum(
        "kgmn,nkd->mkgd", rounded, value_rows, preferred_element_type=jnp.float32
    )
    return (mixed_rows / jnp.transpose(row_total, (2, 0, 1))[..., None]).astype(jnp.bfloat16)


def local(queries, fresh_kv, page_pool, page_host, page_slot, prefix_len, fresh_len):
    stores = lax.axis_size("store")
    block_rows = queries.shape[0]
    head_width = page_pool.shape[3]
    kv_local = head_width // HD
    group_size = queries.shape[1] // head_width
    capacity = max(2, (REQ_HOST * PAGES_MAX + stores - 1) // stores)
    gathered = lax.all_gather(fresh_kv, "tp", axis=1, tiled=True)
    new_kv = lax.dynamic_slice_in_dim(gathered, lax.axis_index("tp") * head_width, head_width, 2)
    buffer, position = plan_requests(page_host, page_slot, prefix_len, stores, capacity)
    arrived = lax.all_to_all(
        jnp.take(
            page_pool,
            lax.all_to_all(buffer, "store", split_axis=0, concat_axis=0, tiled=True),
            axis=0,
        ),
        "store",
        split_axis=0,
        concat_axis=0,
        tiled=True,
    )
    flat_pages = arrived.reshape(stores * capacity, 2, PAGE, head_width)
    fetched = jnp.take(flat_pages, position, axis=0).reshape(
        REQ_HOST, PAGES_MAX, 2, PAGE, head_width
    )
    lengths = fresh_len[0]
    offsets = jnp.cumsum(lengths) - lengths
    positions = jnp.arange(MOST_NEW, dtype=jnp.int32)
    cache_index = jnp.arange(PAGES_MAX * PAGE, dtype=jnp.int32)
    output = jnp.zeros_like(queries)
    for request in range(REQ_HOST):
        offset = offsets[request]
        length = lengths[request]
        window_start = jnp.minimum(offset, block_rows - MOST_NEW)
        q_rows = lax.dynamic_slice_in_dim(queries, window_start, MOST_NEW, 0).reshape(
            MOST_NEW, kv_local, group_size, HD
        )
        new_rows = lax.dynamic_slice_in_dim(new_kv, window_start, MOST_NEW, 1).reshape(
            2, MOST_NEW, kv_local, HD
        )
        cached_keys = fetched[request, :, 0].reshape(PAGES_MAX * PAGE, kv_local, HD)
        cached_values = fetched[request, :, 1].reshape(PAGES_MAX * PAGE, kv_local, HD)
        key_rows = jnp.concatenate([cached_keys, new_rows[0]], axis=0)
        value_rows = jnp.concatenate([cached_values, new_rows[1]], axis=0)
        query_pos = window_start + positions
        cache_ok = jnp.broadcast_to(
            cache_index[None, :] < prefix_len[request], (MOST_NEW, PAGES_MAX * PAGE)
        )
        fresh_ok = (query_pos[None, :] >= offset) & (query_pos[None, :] <= query_pos[:, None])
        key_valid = jnp.concatenate([cache_ok, fresh_ok], axis=1)
        mixed_rows = attend(q_rows, key_rows, value_rows, key_valid).reshape(
            MOST_NEW, queries.shape[1]
        )
        row_ok = (query_pos >= offset) & (query_pos < offset + length)
        old_rows = lax.dynamic_slice_in_dim(output, window_start, MOST_NEW, 0)
        output = lax.dynamic_update_slice_in_dim(
            output, jnp.where(row_ok[:, None], mixed_rows, old_rows), window_start, 0
        )
    return output


def solution(mesh):
    placed = (
        P("store", "tp"),
        P(None, ("store", "tp"), None),
        P("store", None, None, "tp"),
        P("store", None),
        P("store", None),
        P("store"),
        P("store", None),
    )
    return jax.shard_map(
        local, mesh=mesh, in_specs=placed, out_specs=P("store", "tp"), check_vma=False
    )
```

profile of v0, /device:TPU:2, one launch (start us, length us, event | category | flops | bytes accessed | tf_op | source)
XLA Modules:
  0.0 311.5 jit_solution(1080985737066531450)
XLA Ops:
  6.5 0.8 and_select_fusion
  7.5 0.8 reshape.415
  8.5 0.8 broadcast_in_dim.157
  9.4 21.1 %all_to_all.20 = s32[32,1,2]{2,1,0:T(1,128)S(1)} all-to-all(s32[32,1,2]{2,1,0:T(1,128)S(1)} %bitcast.273), channel_id=1, replica_groups=mesh['store'=32,'tp'=8] {'store'}, dimensions={0} | all-to-all | bytes 512 | tf_op jit(solution)/shard_map/all_to_all | solution.py:63
  30.9 5.3 %gather_fusion = bf16[64,2,128,128]{3,2,1,0:T(8,128)(2,1)} fusion(bf16[64,2,128,128]{3,2,1,0:T(8,128)(2,1)} %param.9, s32[1024]{0:T(1024)S(1)} %pad_clamp_fusion.1), kind=kCustom, calls=%fused_computation | custom fusion | bytes 8388864 | tf_op jit(solution)/shard_map/jit(_take)/gather | solution.py:61
  36.2 4.5 %broadcast_select_fusion = bf16[32,2,2,128,128]{4,3,2,1,0:T(8,128)(2,1)} fusion(bf16[32,2,2,128,128]{4,3,2,1,0:T(8,128)(2,1)} %bitcast.255, pred[32,2]{1,0:T(8,128)(4,1)S(1)} %copy.87), kind=kLoop, calls=%fused_computation.42 | loop fusion | flops 2097152 | bytes 8388672 | tf_op jit(solution)/shard_map/jit(_take)/select_n | solution.py:61
  40.7 4.9 %all-to-all-start.1 = ((bf16[32,2,2,128,128]{4,3,2,1,0:T(8,128)(2,1)}), bf16[32,2,2,128,128]{4,3,2,1,0:T(8,128)(2,1)}, u32[]{:S(2)}, u32[]{:S(2)}) async-start(bf16[32,2,2,128,128]{4,3,2,1,0:T(8,128)(2,1)} %broadcast_select_fusion), calls=%async_computation.1 | async-start | bytes 8388608 | tf_op jit(solution)/shard_map/all_to_all | solution.py:60
  45.8 0.5 all-gather.2.cloned.1.call-update
  46.5 0.6 fusion.95
  49.8 2.1 constant_dynamic-slice_fusion
  51.9 2.3 copy.129
  54.3 0.6 fusion.93
  56.3 2.4 copy.128
  59.9 0.7 fusion.94
  60.5 0.7 iota_compare_fusion.2
  61.2 0.6 iota_compare_fusion.3
  61.8 1.2 copy.127
  64.1 0.6 iota_compare_fusion.4
  64.7 1.5 copy.126
  67.5 0.7 iota_compare_fusion.5
  68.2 0.6 compare_and_fusion.4
  68.8 0.6 compare_and_fusion.5
  69.5 0.6 compare_and_fusion.6
  70.0 0.6 compare_and_fusion.9
  71.5 0.3 pad_add_fusion.3
  71.8 0.3 pad_add_fusion.2
  72.4 0.3 pad_add_fusion
  72.7 10.4 %all-gather.2.cloned.1.call-done = bf16[2,1024,1024]{2,1,0:T(8,128)(2,1)} async-done(((bf16[2,128,1024]{2,1,0:T(8,128)(2,1)}), bf16[2,1024,1024]{2,1,0:T(8,128)(2,1)}) %all-gather.2.cloned.1.call-update) | async-done | bytes 4194320 | tf_op jit(solution)/shard_map/all_gather | solution.py:57
  83.1 2.8 dynamic-slice_bitcast_fusion.1
  85.9 0.7 copy.109
  86.7 0.8 copy.103
  87.4 0.7 copy.97
  88.2 0.8 copy.91
  88.9 52.7 %all-to-all-done.1 = bf16[32,2,2,128,128]{4,3,2,1,0:T(8,128)(2,1)} async-done(((bf16[32,2,2,128,128]{4,3,2,1,0:T(8,128)(2,1)}), bf16[32,2,2,128,128]{4,3,2,1,0:T(8,128)(2,1)}, u32[]{:S(2)}, u32[]{:S(2)}) %all-to-all-start.1) | async-done | bytes 4194336 | tf_op jit(solution)/shard_map/all_to_all | solution.py:60
  141.6 4.3 %gather_fusion.1 = bf16[32,2,128,128]{3,2,1,0:T(8,128)(2,1)} fusion(bf16[64,2,128,128]{3,2,1,0:T(8,128)(2,1)} %bitcast.9, s32[1024]{0:T(1024)S(1)} %pad_clamp_fusion), kind=kCustom, calls=%fused_computation.1 | custom fusion | bytes 4194432 | tf_op jit(solution)/shard_map/jit(_take)/gather | solution.py:72
  145.9 1.8 broadcast_select_fusion.1
  147.8 1.2 fusion.92
  148.9 1.8 copy.125
  150.7 9.9 %fusion = (f32[8,384]{1,0:T(8,128)S(1)}, f32[1408,384,8]{1,0,2:T(8,128)}) fusion(pred[384,1408]{0,1:T(8,128)(4,1)S(1)} %pad_add_fusion.3, bf16[384,8,128]{0,2,1:T(8,128)(2,1)} %bitcast.260, bf16[384,1,128]{2,0,1:T(8,128)(2,1)} %get-tuple-element.9, bf16[1024,1,128]{2,0,1:T(8,128)(2,1)} %bitcast.264), kind=kOutput, calls=%fused_computation.4 | convolution fusion | flops 1120990208 | bytes 19001344 | tf_op jit(solution)/shard_map/mkgd,nkd->kgmn/dot_general | solution.py:37
  160.6 9.8 %fusion.18 = f32[8,384]{1,0:T(8,128)S(1)} fusion(f32[1408,384,8]{1,0,2:T(8,128)} %get-tuple-element.44, f32[8,384]{1,0:T(8,128)S(1)} %get-tuple-element.43, pred[384,1408]{0,1:T(8,128)(4,1)S(1)} %pad_add_fusion.3), kind=kLoop, calls=%fused_computation.28 | loop fusion | flops 17298432 | bytes 17866752 | tf_op jit(solution)/shard_map/reduce_sum | solution.py:42
  170.5 10.7 %fusion.36 = bf16[384,1,8,128]{0,3,2,1:T(8,128)(2,1)} fusion(f32[1408,384,8]{1,0,2:T(8,128)} %get-tuple-element.44, f32[8,384]{1,0:T(8,128)S(1)} %get-tuple-element.43, pred[384,1408]{0,1:T(8,128)(4,1)S(1)} %pad_add_fusion.3, f32[384,8]{0,1:T(8,128)S(1)} %bitcast.274, bf16[384,1,128]{0,2,1:T(8,128)(2,1)} %copy.109, bf16[1024,1,128]{0,2,1:T(8,128)(2,1)} %copy.125), kind=kOutput, calls=%fused_computation.49 | convolution fusion | flops 1126105088 | bytes 19013632 | tf_op jit(solution)/shard_map/kgmn,nkd->mkgd/dot_general | solution.py:44
  181.1 2.3 copy.113
  183.4 1.8 copy.124
  185.2 9.9 %fusion.3 = (f32[8,384]{1,0:T(8,128)S(1)}, f32[1408,384,8]{1,0,2:T(8,128)}) fusion(pred[384,1408]{0,1:T(8,128)(4,1)S(1)} %pad_add_fusion.2, bf16[384,8,128]{0,2,1:T(8,128)(2,1)} %bitcast.259, bf16[384,1,128]{2,0,1:T(8,128)(2,1)} %get-tuple-element.10, bf16[1024,1,128]{2,0,1:T(8,128)(2,1)} %bitcast.263), kind=kOutput, calls=%fused_computation.9 | convolution fusion | flops 1120990208 | bytes 19001344 | tf_op jit(solution)/shard_map/mkgd,nkd->kgmn/dot_general | solution.py:37
  195.2 9.4 %fusion.16 = f32[8,384]{1,0:T(8,128)S(1)} fusion(f32[1408,384,8]{1,0,2:T(8,128)} %get-tuple-element.42, f32[8,384]{1,0:T(8,128)S(1)} %get-tuple-element.41, pred[384,1408]{0,1:T(8,128)(4,1)S(1)} %pad_add_fusion.2), kind=kLoop, calls=%fused_computation.26 | loop fusion | flops 17298432 | bytes 17866752 | tf_op jit(solution)/shard_map/reduce_sum | solution.py:42
  204.6 10.8 %fusion.37 = bf16[384,1,8,128]{0,3,2,1:T(8,128)(2,1)} fusion(f32[1408,384,8]{1,0,2:T(8,128)} %get-tuple-element.42, f32[8,384]{1,0:T(8,128)S(1)} %get-tuple-element.41, pred[384,1408]{0,1:T(8,128)(4,1)S(1)} %pad_add_fusion.2, f32[384,8]{0,1:T(8,128)S(1)} %bitcast.275, bf16[384,1,128]{0,2,1:T(8,128)(2,1)S(1)} %copy-done.9, bf16[1024,1,128]{0,2,1:T(8,128)(2,1)} %copy.124), kind=kOutput, calls=%fused_computation.51 | convolution fusion | flops 1126105088 | bytes 19013632 | tf_op jit(solution)/shard_map/kgmn,nkd->mkgd/dot_general | solution.py:44
  215.4 2.3 copy.107
  217.8 0.8 copy.123
  218.6 8.9 %fusion.6 = (f32[8,384]{1,0:T(8,128)S(1)}, f32[1408,384,8]{1,0,2:T(8,128)}) fusion(pred[384,1408]{0,1:T(8,128)(4,1)S(1)} %pad_add_fusion.1, bf16[384,8,128]{0,2,1:T(8,128)(2,1)} %bitcast.258, bf16[384,1,128]{2,0,1:T(8,128)(2,1)S(1)} %copy-done.6, bf16[1024,1,128]{2,0,1:T(8,128)(2,1)S(1)} %bitcast.262), kind=kOutput, calls=%fused_computation.14 | convolution fusion | flops 1120990208 | bytes 19001344 | tf_op jit(solution)/shard_map/mkgd,nkd->kgmn/dot_general | solution.py:37
  227.5 9.5 %fusion.14 = f32[8,384]{1,0:T(8,128)S(1)} fusion(f32[1408,384,8]{1,0,2:T(8,128)} %get-tuple-element.40, f32[8,384]{1,0:T(8,128)S(1)} %get-tuple-element.39, pred[384,1408]{0,1:T(8,128)(4,1)S(1)} %pad_add_fusion.1), kind=kLoop, calls=%fused_computation.24 | loop fusion | flops 17298432 | bytes 17866752 | tf_op jit(solution)/shard_map/reduce_sum | solution.py:42
  237.0 9.7 %fusion.38 = bf16[384,1,8,128]{0,3,2,1:T(8,128)(2,1)S(1)} fusion(f32[1408,384,8]{1,0,2:T(8,128)} %get-tuple-element.40, f32[8,384]{1,0:T(8,128)S(1)} %get-tuple-element.39, pred[384,1408]{0,1:T(8,128)(4,1)S(1)} %pad_add_fusion.1, f32[384,8]{0,1:T(8,128)S(1)} %bitcast.276, bf16[384,1,128]{0,2,1:T(8,128)(2,1)S(1)} %copy-done.8, bf16[1024,1,128]{0,2,1:T(8,128)(2,1)} %copy.123), kind=kOutput, calls=%fused_computation.53 | convolution fusion | flops 1126105088 | bytes 19013632 | tf_op jit(solution)/shard_map/kgmn,nkd->mkgd/dot_general | solution.py:44
  246.7 1.2 copy.101
  248.1 7.9 %fusion.9 = (f32[8,384]{1,0:T(8,128)S(1)}, f32[1408,384,8]{1,0,2:T(8,128)}) fusion(pred[384,1408]{0,1:T(8,128)(4,1)S(1)} %pad_add_fusion, bf16[384,8,128]{0,2,1:T(8,128)(2,1)S(1)} %bitcast.257, bf16[384,1,128]{2,0,1:T(8,128)(2,1)S(1)} %copy-done.5, bf16[1024,1,128]{2,0,1:T(8,128)(2,1)S(1)} %bitcast.261), kind=kOutput, calls=%fused_computation.19 | convolution fusion | flops 1120990208 | bytes 19001344 | tf_op jit(solution)/shard_map/mkgd,nkd->kgmn/dot_general | solution.py:37
  256.0 9.4 %fusion.12 = f32[8,384]{1,0:T(8,128)S(1)} fusion(f32[1408,384,8]{1,0,2:T(8,128)} %get-tuple-element.38, f32[8,384]{1,0:T(8,128)S(1)} %get-tuple-element.37, pred[384,1408]{0,1:T(8,128)(4,1)S(1)} %pad_add_fusion), kind=kLoop, calls=%fused_computation.22 | loop fusion | flops 17298432 | bytes 17866752 | tf_op jit(solution)/shard_map/reduce_sum | solution.py:42
  265.5 9.7 %fusion.39 = bf16[384,1,8,128]{0,3,2,1:T(8,128)(2,1)S(1)} fusion(f32[1408,384,8]{1,0,2:T(8,128)} %get-tuple-element.38, f32[8,384]{1,0:T(8,128)S(1)} %get-tuple-element.37, pred[384,1408]{0,1:T(8,128)(4,1)S(1)} %pad_add_fusion, f32[384,8]{0,1:T(8,128)S(1)} %bitcast.277, bf16[384,1,128]{0,2,1:T(8,128)(2,1)S(1)} %copy-done.7, bf16[1024,1,128]{0,2,1:T(8,128)(2,1)S(1)} %copy.122), kind=kOutput, calls=%fused_computation.55 | convolution fusion | flops 1126105088 | bytes 19013632 | tf_op jit(solution)/shard_map/kgmn,nkd->mkgd/dot_general | solution.py:44
  275.2 0.3 copy.95
  275.5 1.0 broadcast_select_fusion.2
  276.7 5.6 %dynamic_update_slice.12 = bf16[1024,1024]{1,0:T(8,128)(2,1)S(1)} dynamic-update-slice(bf16[1024,1024]{1,0:T(8,128)(2,1)S(1)} %broadcast_in_dim.152, bf16[384,1024]{1,0:T(8,128)(2,1)} %broadcast_select_fusion.2, s32[]{:T(128)S(6)} %select_n.157, s32[]{:T(128)} %constant.116.clone.1) | dynamic-update-slice | bytes 1572868 | tf_op jit(solution)/shard_map/dynamic_update_slice | solution.py:105
  282.3 2.3 dynamic-slice_select_fusion.2
  284.7 5.5 %dynamic_update_slice.13 = bf16[1024,1024]{1,0:T(8,128)(2,1)S(1)} dynamic-update-slice(bf16[1024,1024]{1,0:T(8,128)(2,1)S(1)} %dynamic_update_slice.12, bf16[384,1024]{1,0:T(8,128)(2,1)} %dynamic-slice_select_fusion.2, s32[]{:T(128)S(6)} %select_n.164, s32[]{:T(128)} %constant.116.clone.1) | dynamic-update-slice | bytes 1572868 | tf_op jit(solution)/shard_map/dynamic_update_slice | solution.py:105
  290.2 2.3 dynamic-slice_select_fusion.1
  292.6 5.5 %dynamic_update_slice.14 = bf16[1024,1024]{1,0:T(8,128)(2,1)S(1)} dynamic-update-slice(bf16[1024,1024]{1,0:T(8,128)(2,1)S(1)} %dynamic_update_slice.13, bf16[384,1024]{1,0:T(8,128)(2,1)} %dynamic-slice_select_fusion.1, s32[]{:T(128)S(6)} %select_n.169, s32[]{:T(128)} %constant.116.clone.1) | dynamic-update-slice | bytes 1572868 | tf_op jit(solution)/shard_map/dynamic_update_slice | solution.py:105
  298.2 1.5 dynamic-slice_select_fusion
  299.7 4.7 %dynamic_update_slice.15 = bf16[1024,1024]{1,0:T(8,128)(2,1)} dynamic-update-slice(bf16[1024,1024]{1,0:T(8,128)(2,1)} %copy-done, bf16[384,1024]{1,0:T(8,128)(2,1)} %dynamic-slice_select_fusion, s32[]{:T(128)S(6)} %select_n.174, s32[]{:T(128)} %constant.116.clone.1) | dynamic-update-slice | bytes 1572868 | tf_op jit(solution)/shard_map/dynamic_update_slice | solution.py:105
  (64 shorter events, 3.2 us)
Async XLA Ops:
  6.5 47.7 %copy-start.10 = (s32[4,8]{1,0:T(4,128)S(1)}, s32[4,8]{1,0:T(4,128)}, u32[]{:S(2)}) copy-start(s32[4,8]{1,0:T(4,128)} %param.10) | copy-start | bytes 388
  6.5 39.8 %copy-start.11 = (s32[1,4]{1,0:T(1,128)S(1)}, s32[1,4]{1,0:T(1,128)}, u32[]{:S(2)}) copy-start(s32[1,4]{1,0:T(1,128)} %param.13) | copy-start | bytes 52
  6.5 43.3 %copy-start.1 = (bf16[1024,1024]{1,0:T(8,128)(2,1)S(1)}, bf16[1024,1024]{1,0:T(8,128)(2,1)}, u32[]{:S(2)}) copy-start(bf16[1024,1024]{1,0:T(8,128)(2,1)} %param.7) | copy-start | bytes 6291460
  30.9 28.9 %copy-start.12 = (s32[4]{0:T(128)S(1)}, s32[4]{0:T(128)}, u32[]{:S(2)}) copy-start(s32[4]{0:T(128)} %param.12) | copy-start | bytes 52
  40.7 100.9 %all-to-all-start.1 = ((bf16[32,2,2,128,128]{4,3,2,1,0:T(8,128)(2,1)}), bf16[32,2,2,128,128]{4,3,2,1,0:T(8,128)(2,1)}, u32[]{:S(2)}, u32[]{:S(2)}) async-start(bf16[32,2,2,128,128]{4,3,2,1,0:T(8,128)(2,1)} %broadcast_select_fusion), calls=%async_computation.1 | async-start | bytes 8388608 | tf_op jit(solution)/shard_map/all_to_all | solution.py:60
  45.6 37.5 %all-gather.2.cloned.1.call-start = ((), (), s32[]{:S(2)}) async-start(), calls=%async_computation.2 | async-start | bytes 4718592 | tf_op jit(solution)/shard_map/all_gather | solution.py:57
  185.2 19.4 %copy-start.9 = (bf16[384,1,128]{0,2,1:T(8,128)(2,1)S(1)}, bf16[384,1,128]{0,2,1:T(8,128)(2,1)}, u32[]{:S(2)}) copy-start(bf16[384,1,128]{0,2,1:T(8,128)(2,1)} %copy.103) | copy-start | bytes 294916
  204.6 13.2 %copy-start.4 = (bf16[1,8,1,128,128]{4,3,2,1,0:T(8,128)(2,1)S(1)}, bf16[1,8,1,128,128]{4,3,2,1,0:T(8,128)(2,1)}, u32[]{:S(2)}) copy-start(bf16[1,8,1,128,128]{4,3,2,1,0:T(8,128)(2,1)} %get-tuple-element.18) | copy-start | bytes 786436
  204.6 14.0 %copy-start.6 = (bf16[384,1,128]{2,0,1:T(8,128)(2,1)S(1)}, bf16[384,1,128]{2,0,1:T(8,128)(2,1)}, u32[]{:S(2)}) copy-start(bf16[384,1,128]{2,0,1:T(8,128)(2,1)} %get-tuple-element.11) | copy-start | bytes 294916
  227.5 9.5 %copy-start.8 = (bf16[384,1,128]{0,2,1:T(8,128)(2,1)S(1)}, bf16[384,1,128]{0,2,1:T(8,128)(2,1)}, u32[]{:S(2)}) copy-start(bf16[384,1,128]{0,2,1:T(8,128)(2,1)} %copy.97) | copy-start | bytes 294916
  237.0 11.0 %copy-start.3 = (bf16[1,8,1,128,128]{4,3,2,1,0:T(8,128)(2,1)S(1)}, bf16[1,8,1,128,128]{4,3,2,1,0:T(8,128)(2,1)}, u32[]{:S(2)}) copy-start(bf16[1,8,1,128,128]{4,3,2,1,0:T(8,128)(2,1)} %get-tuple-element.20) | copy-start | bytes 786436
  237.0 11.1 %copy-start.5 = (bf16[384,1,128]{2,0,1:T(8,128)(2,1)S(1)}, bf16[384,1,128]{2,0,1:T(8,128)(2,1)}, u32[]{:S(2)}) copy-start(bf16[384,1,128]{2,0,1:T(8,128)(2,1)} %get-tuple-element.12) | copy-start | bytes 294916
  248.1 17.4 %copy-start.7 = (bf16[384,1,128]{0,2,1:T(8,128)(2,1)S(1)}, bf16[384,1,128]{0,2,1:T(8,128)(2,1)}, u32[]{:S(2)}) copy-start(bf16[384,1,128]{0,2,1:T(8,128)(2,1)} %copy.91) | copy-start | bytes 294916
  265.5 32.7 %copy-start.2 = (bf16[384,1024]{1,0:T(8,128)(2,1)S(1)}, bf16[384,1024]{1,0:T(8,128)(2,1)}, u32[]{:S(2)}) copy-start(bf16[384,1024]{1,0:T(8,128)(2,1)} %copy.113) | copy-start | bytes 2359300
  298.1 1.6 copy-start
Sparse Core Ops, SparseCore 0:
  48.3 34.8 all-gather.1
where the time goes:
time: 315 us; the launch traced here: 311 us
  matrix products  77.5 us (25%)
  waiting for transfers between devices  63.6 us (20%)
  local copies, waits for them, and re-layouts  62.7 us (20%)
  other arithmetic  60 us (19%)
  between operations  21.5 us (7%)
  blocking collectives  21.1 us (7%)
  starting transfers between devices  5.07 us (2%)
    all_to_all x1, waiting for transfers between devices, local(): lax.all_to_all(jnp.take(page_pool, lax.all_to_all(buffer, 'store', split_...  52.7 us
    dot_general x4, matrix products, attend(): jnp.einsum('kgmn,nkd->mkgd', rounded, value_rows, preferred_element_type=...  40.9 us
    reduce_sum x4, other arithmetic, attend(): row_total = jnp.sum(weights, axis=-1)  38.1 us
    dot_general x4, matrix products, attend(): jnp.einsum('mkgd,nkd->kgmn', q_rows, key_rows, preferred_element_type=jnp...  36.7 us
    dynamic_update_slice x4, local copies, waits for them, and re-layouts, local(): lax.dynamic_update_slice_in_dim(output, jnp.where(row_ok[:, None], mixed_...  21.4 us
    all_to_all x1, blocking collectives, local(): lax.all_to_all(buffer, 'store', split_axis=0, concat_axis=0, tiled=True)  21.1 us
    all_gather x1, waiting for transfers between devices, local(): gathered = lax.all_gather(fresh_kv, 'tp', axis=1, tiled=True)  10.4 us
    unnamed x30, local copies, waits for them, and re-layouts  7.46 us
  transfers between devices with their start and end apart: 2, of which 2 were waited for; matrix products, arithmetic and copies ran while one was open for 8% of the time, Pallas kernels for 0%

commit v1 on v0

--- a/solution.py
+++ b/solution.py
@@ -54,7 +54,12 @@
     kv_local = head_width // HD
     group_size = queries.shape[1] // head_width
     capacity = max(2, (REQ_HOST * PAGES_MAX + stores - 1) // stores)
-    gathered = lax.all_gather(fresh_kv, "tp", axis=1, tiled=True)
+    ring = [fresh_kv]
+    for hop in range(7):
+        ring.append(lax.ppermute(ring[-1], "tp", [(dev, (dev + 1) % 8) for dev in range(8)]))
+    gathered = jnp.roll(
+        jnp.concatenate(ring[::-1], axis=1), (lax.axis_index("tp") + 1) * ring[0].shape[1], axis=1
+    )
     new_kv = lax.dynamic_slice_in_dim(gathered, lax.axis_index("tp") * head_width, head_width, 2)
     buffer, position = plan_requests(page_host, page_slot, prefix_len, stores, capacity)
     arrived = lax.all_to_all(

time: 315 us -> 305 us (0.968)
  waiting for transfers between devices: 63.6 us -> 45.8 us
  between operations: 21.5 us -> 8.24 us
  local copies, waits for them, and re-layouts: 62.7 us -> 75.1 us
  other arithmetic: 60 us -> 63.2 us
  starting transfers between devices: 5.07 us -> 8.26 us
    all_to_all x1, waiting for transfers between devices: 52.7 us -> 12.6 us  [local(): lax.all_to_all(jnp.take(page_pool, lax.all_to_all(buffer, 'store', split_...]
    ppermute x0 -> x7, waiting for transfers between devices: none -> 33.2 us  [local(): lax.ppermute(ring[-1], 'tp', [(dev, (dev + 1) % 8) for dev in range(8)])]
    unnamed x30 -> x55, local copies, waits for them, and re-layouts: 7.46 us -> 20.1 us
    all_gather x1 -> x0, waiting for transfers between devices: 10.4 us -> none  [local(): gathered = lax.all_gather(fresh_kv, 'tp', axis=1, tiled=True)]
    ppermute x0 -> x7, starting transfers between devices: none -> 3.23 us  [local(): lax.ppermute(ring[-1], 'tp', [(dev, (dev + 1) % 8) for dev in range(8)])]
  transfers between devices with their start and end apart: 2 -> 8, of which waited for: 2 -> 6; matrix products, arithmetic and copies ran while one was open for 8% -> 13% of each run, Pallas kernels for 0% -> 0%
where the time goes in v1:
time: 305 us; the launch traced here: 300 us
  matrix products  78.4 us (26%)
  local copies, waits for them, and re-layouts  75.1 us (25%)
  other arithmetic  63.2 us (21%)
  waiting for transfers between devices  45.8 us (15%)
  blocking collectives  21.1 us (7%)
  starting transfers between devices  8.26 us (3%)
  between operations  8.24 us (3%)
    dot_general x4, matrix products, attend(): jnp.einsum('kgmn,nkd->mkgd', rounded, value_rows, preferred_element_type=...  41.7 us
    reduce_sum x4, other arithmetic, attend(): row_total = jnp.sum(weights, axis=-1)  38.2 us
    dot_general x4, matrix products, attend(): jnp.einsum('mkgd,nkd->kgmn', q_rows, key_rows, preferred_element_type=jnp...  36.7 us
    ppermute x7, waiting for transfers between devices, local(): lax.ppermute(ring[-1], 'tp', [(dev, (dev + 1) % 8) for dev in range(8)])  33.2 us
    dynamic_update_slice x4, local copies, waits for them, and re-layouts, local(): lax.dynamic_update_slice_in_dim(output, jnp.where(row_ok[:, None], mixed_...  21.4 us
    all_to_all x1, blocking collectives, local(): lax.all_to_all(buffer, 'store', split_axis=0, concat_axis=0, tiled=True)  21.1 us
    unnamed x55, local copies, waits for them, and re-layouts  20.1 us
    all_to_all x1, waiting for transfers between devices, local(): lax.all_to_all(jnp.take(page_pool, lax.all_to_all(buffer, 'store', split_...  12.6 us
  transfers between devices with their start and end apart: 8, of which 6 were waited for; matrix products, arithmetic and copies ran while one was open for 13% of the time, Pallas kernels for 0%

profile of v1, /device:TPU:2, one launch (start us, length us, event | category | flops | bytes accessed | tf_op | source)
XLA Modules:
  0.0 300.1 jit_solution(17667374048298610260)
XLA Ops:
  2.8 21.1 %all_to_all.20 = s32[32,1,2]{2,1,0:T(1,128)S(1)} all-to-all(s32[32,1,2]{2,1,0:T(1,128)S(1)} %bitcast.273), channel_id=1, replica_groups=mesh['store'=32,'tp'=8] {'store'}, dimensions={0} | all-to-all | bytes 512 | tf_op jit(solution)/shard_map/all_to_all | solution.py:68
  24.2 5.3 %gather_fusion = bf16[64,2,128,128]{3,2,1,0:T(8,128)(2,1)} fusion(bf16[64,2,128,128]{3,2,1,0:T(8,128)(2,1)} %param.9, s32[1024]{0:T(1024)S(1)} %pad_clamp_fusion.1), kind=kCustom, calls=%fused_computation | custom fusion | bytes 8388864 | tf_op jit(solution)/shard_map/jit(_take)/gather | solution.py:66
  29.5 4.7 %broadcast_select_fusion = bf16[32,2,2,128,128]{4,3,2,1,0:T(8,128)(2,1)} fusion(bf16[32,2,2,128,128]{4,3,2,1,0:T(8,128)(2,1)} %bitcast.255, pred[32,2]{1,0:T(8,128)(4,1)S(1)} %copy.87), kind=kLoop, calls=%fused_computation.42 | loop fusion | flops 2097152 | bytes 8388672 | tf_op jit(solution)/shard_map/jit(_take)/select_n | solution.py:66
  34.2 5.0 %all-to-all-start.1 = ((bf16[32,2,2,128,128]{4,3,2,1,0:T(8,128)(2,1)}), bf16[32,2,2,128,128]{4,3,2,1,0:T(8,128)(2,1)}, u32[]{:S(2)}, u32[]{:S(2)}) async-start(bf16[32,2,2,128,128]{4,3,2,1,0:T(8,128)(2,1)} %broadcast_select_fusion), calls=%async_computation.1 | async-start | bytes 8388608 | tf_op jit(solution)/shard_map/all_to_all | solution.py:65
  50.4 2.1 constant_dynamic-slice_fusion
  53.2 1.6 collective-permute-start.1
  55.7 6.3 %collective-permute-done.1 = bf16[2,128,1024]{2,1,0:T(8,128)(2,1)S(1)} collective-permute-done((bf16[2,128,1024]{2,1,0:T(8,128)(2,1)}, bf16[2,128,1024]{2,1,0:T(8,128)(2,1)S(1)}, u32[]{:S(2)}, u32[]{:S(2)}) %collective-permute-start.1) | collective-permute-done | bytes 524320 | tf_op jit(solution)/shard_map/ppermute | solution.py:59
  62.7 0.9 compare_and_fusion.2
  63.6 0.8 compare_and_fusion.3
  64.4 6.2 %collective-permute-done.2 = bf16[2,128,1024]{2,1,0:T(8,128)(2,1)S(1)} collective-permute-done((bf16[2,128,1024]{2,1,0:T(8,128)(2,1)S(1)}, bf16[2,128,1024]{2,1,0:T(8,128)(2,1)S(1)}, u32[]{:S(2)}, u32[]{:S(2)}) %collective-permute-start.2) | collective-permute-done | bytes 524320 | tf_op jit(solution)/shard_map/ppermute | solution.py:59
  71.6 7.7 %collective-permute-done.3 = bf16[2,128,1024]{2,1,0:T(8,128)(2,1)S(1)} collective-permute-done((bf16[2,128,1024]{2,1,0:T(8,128)(2,1)S(1)}, bf16[2,128,1024]{2,1,0:T(8,128)(2,1)S(1)}, u32[]{:S(2)}, u32[]{:S(2)}) %collective-permute-start.3) | collective-permute-done | bytes 524320 | tf_op jit(solution)/shard_map/ppermute | solution.py:59
  79.3 0.8 copy-done.7
  80.9 7.1 %collective-permute-done.4 = bf16[2,128,1024]{2,1,0:T(8,128)(2,1)} collective-permute-done((bf16[2,128,1024]{2,1,0:T(8,128)(2,1)S(1)}, bf16[2,128,1024]{2,1,0:T(8,128)(2,1)}, u32[]{:S(2)}, u32[]{:S(2)}) %collective-permute-start.4) | collective-permute-done | bytes 524320 | tf_op jit(solution)/shard_map/ppermute | solution.py:59
  88.6 2.3 copy.129
  90.9 2.3 copy.128
  93.2 1.2 copy.127
  94.3 1.5 copy.126
  95.9 1.2 pad_add_fusion.1
  97.1 1.6 collective-permute-start.6
  98.7 1.2 pad_add_fusion
  99.9 5.9 %collective-permute-done.6 = bf16[2,128,1024]{2,1,0:T(8,128)(2,1)S(1)} collective-permute-done((bf16[2,128,1024]{2,1,0:T(8,128)(2,1)}, bf16[2,128,1024]{2,1,0:T(8,128)(2,1)S(1)}, u32[]{:S(2)}, u32[]{:S(2)}) %collective-permute-start.6) | collective-permute-done | bytes 524320 | tf_op jit(solution)/shard_map/ppermute | solution.py:59
  105.9 1.1 constant_dynamic-update-slice_fusion.14
  107.0 1.1 constant_dynamic-update-slice_fusion.13
  108.1 1.1 constant_dynamic-update-slice_fusion.12
  109.2 1.1 constant_dynamic-update-slice_fusion.11
  110.3 1.1 constant_dynamic-update-slice_fusion.10
  111.3 1.1 constant_dynamic-update-slice_fusion.9
  112.5 1.1 constant_dynamic-update-slice_fusion.6
  113.6 1.1 constant_dynamic-update-slice_fusion.5
  114.7 1.1 constant_dynamic-update-slice_fusion.4
  115.8 1.1 constant_dynamic-update-slice_fusion.2
  116.9 1.1 constant_dynamic-update-slice_fusion.1
  118.0 1.5 dynamic-slice_bitcast_fusion.1
  122.5 12.6 %all-to-all-done.1 = bf16[32,2,2,128,128]{4,3,2,1,0:T(8,128)(2,1)} async-done(((bf16[32,2,2,128,128]{4,3,2,1,0:T(8,128)(2,1)}), bf16[32,2,2,128,128]{4,3,2,1,0:T(8,128)(2,1)}, u32[]{:S(2)}, u32[]{:S(2)}) %all-to-all-start.1) | async-done | bytes 4194336 | tf_op jit(solution)/shard_map/all_to_all | solution.py:65
  135.1 4.3 %gather_fusion.1 = bf16[32,2,128,128]{3,2,1,0:T(8,128)(2,1)} fusion(bf16[64,2,128,128]{3,2,1,0:T(8,128)(2,1)} %bitcast.9, s32[1024]{0:T(1024)S(1)} %pad_clamp_fusion), kind=kCustom, calls=%fused_computation.1 | custom fusion | bytes 4194432 | tf_op jit(solution)/shard_map/jit(_take)/gather | solution.py:77
  139.4 1.8 broadcast_select_fusion.1
  141.3 1.2 fusion.92
  142.4 1.8 copy.125
  144.2 9.9 %fusion = (f32[8,384]{1,0:T(8,128)S(1)}, f32[1408,384,8]{1,0,2:T(8,128)}) fusion(pred[384,1408]{0,1:T(8,128)(4,1)S(1)} %pad_add_fusion.3, bf16[384,8,128]{0,2,1:T(8,128)(2,1)} %bitcast.260, bf16[384,1,128]{2,0,1:T(8,128)(2,1)} %get-tuple-element.9, bf16[1024,1,128]{2,0,1:T(8,128)(2,1)} %bitcast.264), kind=kOutput, calls=%fused_computation.4 | convolution fusion | flops 1120990208 | bytes 19001344 | tf_op jit(solution)/shard_map/mkgd,nkd->kgmn/dot_general | solution.py:37
  154.2 9.8 %fusion.18 = f32[8,384]{1,0:T(8,128)S(1)} fusion(f32[1408,384,8]{1,0,2:T(8,128)} %get-tuple-element.44, f32[8,384]{1,0:T(8,128)S(1)} %get-tuple-element.43, pred[384,1408]{0,1:T(8,128)(4,1)S(1)} %pad_add_fusion.3), kind=kLoop, calls=%fused_computation.28 | loop fusion | flops 17298432 | bytes 17866752 | tf_op jit(solution)/shard_map/reduce_sum | solution.py:42
  164.0 10.6 %fusion.36 = bf16[384,1,8,128]{0,3,2,1:T(8,128)(2,1)} fusion(f32[1408,384,8]{1,0,2:T(8,128)} %get-tuple-element.44, f32[8,384]{1,0:T(8,128)S(1)} %get-tuple-element.43, pred[384,1408]{0,1:T(8,128)(4,1)S(1)} %pad_add_fusion.3, f32[384,8]{0,1:T(8,128)S(1)} %bitcast.274, bf16[384,1,128]{0,2,1:T(8,128)(2,1)} %copy.109, bf16[1024,1,128]{0,2,1:T(8,128)(2,1)} %copy.125), kind=kOutput, calls=%fused_computation.49 | convolution fusion | flops 1126105088 | bytes 19013632 | tf_op jit(solution)/shard_map/kgmn,nkd->mkgd/dot_general | solution.py:44
  174.6 2.3 copy.113
  176.9 1.8 copy.124
  178.7 9.9 %fusion.3 = (f32[8,384]{1,0:T(8,128)S(1)}, f32[1408,384,8]{1,0,2:T(8,128)}) fusion(pred[384,1408]{0,1:T(8,128)(4,1)S(1)} %pad_add_fusion.2, bf16[384,8,128]{0,2,1:T(8,128)(2,1)} %bitcast.259, bf16[384,1,128]{2,0,1:T(8,128)(2,1)} %get-tuple-element.10, bf16[1024,1,128]{2,0,1:T(8,128)(2,1)} %bitcast.263), kind=kOutput, calls=%fused_computation.9 | convolution fusion | flops 1120990208 | bytes 19001344 | tf_op jit(solution)/shard_map/mkgd,nkd->kgmn/dot_general | solution.py:37
  188.7 9.5 %fusion.16 = f32[8,384]{1,0:T(8,128)S(1)} fusion(f32[1408,384,8]{1,0,2:T(8,128)} %get-tuple-element.42, f32[8,384]{1,0:T(8,128)S(1)} %get-tuple-element.41, pred[384,1408]{0,1:T(8,128)(4,1)S(1)} %pad_add_fusion.2), kind=kLoop, calls=%fused_computation.26 | loop fusion | flops 17298432 | bytes 17866752 | tf_op jit(solution)/shard_map/reduce_sum | solution.py:42
  198.1 10.8 %fusion.37 = bf16[384,1,8,128]{0,3,2,1:T(8,128)(2,1)} fusion(f32[1408,384,8]{1,0,2:T(8,128)} %get-tuple-element.42, f32[8,384]{1,0:T(8,128)S(1)} %get-tuple-element.41, pred[384,1408]{0,1:T(8,128)(4,1)S(1)} %pad_add_fusion.2, f32[384,8]{0,1:T(8,128)S(1)} %bitcast.275, bf16[384,1,128]{0,2,1:T(8,128)(2,1)S(1)} %copy-done.14, bf16[1024,1,128]{0,2,1:T(8,128)(2,1)} %copy.124), kind=kOutput, calls=%fused_computation.51 | convolution fusion | flops 1126105088 | bytes 19013632 | tf_op jit(solution)/shard_map/kgmn,nkd->mkgd/dot_general | solution.py:44
  208.9 2.3 copy.107
  211.3 0.8 copy.123
  212.1 8.9 %fusion.6 = (f32[8,384]{1,0:T(8,128)S(1)}, f32[1408,384,8]{1,0,2:T(8,128)}) fusion(pred[384,1408]{0,1:T(8,128)(4,1)S(1)} %pad_add_fusion.1, bf16[384,8,128]{0,2,1:T(8,128)(2,1)} %bitcast.258, bf16[384,1,128]{2,0,1:T(8,128)(2,1)S(1)} %copy-done.11, bf16[1024,1,128]{2,0,1:T(8,128)(2,1)S(1)} %bitcast.262), kind=kOutput, calls=%fused_computation.14 | convolution fusion | flops 1120990208 | bytes 19001344 | tf_op jit(solution)/shard_map/mkgd,nkd->kgmn/dot_general | solution.py:37
  221.0 9.5 %fusion.14 = f32[8,384]{1,0:T(8,128)S(1)} fusion(f32[1408,384,8]{1,0,2:T(8,128)} %get-tuple-element.40, f32[8,384]{1,0:T(8,128)S(1)} %get-tuple-element.39, pred[384,1408]{0,1:T(8,128)(4,1)S(1)} %pad_add_fusion.1), kind=kLoop, calls=%fused_computation.24 | loop fusion | flops 17298432 | bytes 17866752 | tf_op jit(solution)/shard_map/reduce_sum | solution.py:42
  230.5 9.7 %fusion.38 = bf16[384,1,8,128]{0,3,2,1:T(8,128)(2,1)S(1)} fusion(f32[1408,384,8]{1,0,2:T(8,128)} %get-tuple-element.40, f32[8,384]{1,0:T(8,128)S(1)} %get-tuple-element.39, pred[384,1408]{0,1:T(8,128)(4,1)S(1)} %pad_add_fusion.1, f32[384,8]{0,1:T(8,128)S(1)} %bitcast.276, bf16[384,1,128]{0,2,1:T(8,128)(2,1)S(1)} %copy-done.13, bf16[1024,1,128]{0,2,1:T(8,128)(2,1)} %copy.123), kind=kOutput, calls=%fused_computation.53 | convolution fusion | flops 1126105088 | bytes 19013632 | tf_op jit(solution)/shard_map/kgmn,nkd->mkgd/dot_general | solution.py:44
  240.2 1.2 copy.101
  241.6 7.9 %fusion.9 = (f32[8,384]{1,0:T(8,128)S(1)}, f32[1408,384,8]{1,0,2:T(8,128)}) fusion(pred[384,1408]{0,1:T(8,128)(4,1)S(1)} %pad_add_fusion, bf16[384,8,128]{0,2,1:T(8,128)(2,1)S(1)} %bitcast.257, bf16[384,1,128]{2,0,1:T(8,128)(2,1)S(1)} %copy-done.10, bf16[1024,1,128]{2,0,1:T(8,128)(2,1)S(1)} %bitcast.261), kind=kOutput, calls=%fused_computation.19 | convolution fusion | flops 1120990208 | bytes 19001344 | tf_op jit(solution)/shard_map/mkgd,nkd->kgmn/dot_general | solution.py:37
  249.5 9.5 %fusion.12 = f32[8,384]{1,0:T(8,128)S(1)} fusion(f32[1408,384,8]{1,0,2:T(8,128)} %get-tuple-element.38, f32[8,384]{1,0:T(8,128)S(1)} %get-tuple-element.37, pred[384,1408]{0,1:T(8,128)(4,1)S(1)} %pad_add_fusion), kind=kLoop, calls=%fused_computation.22 | loop fusion | flops 17298432 | bytes 17866752 | tf_op jit(solution)/shard_map/reduce_sum | solution.py:42
  259.0 10.5 %fusion.39 = bf16[384,1,8,128]{0,3,2,1:T(8,128)(2,1)} fusion(f32[1408,384,8]{1,0,2:T(8,128)} %get-tuple-element.38, f32[8,384]{1,0:T(8,128)S(1)} %get-tuple-element.37, pred[384,1408]{0,1:T(8,128)(4,1)S(1)} %pad_add_fusion, f32[384,8]{0,1:T(8,128)S(1)} %bitcast.277, bf16[384,1,128]{0,2,1:T(8,128)(2,1)S(1)} %copy-done.12, bf16[1024,1,128]{0,2,1:T(8,128)(2,1)S(1)} %copy.122), kind=kOutput, calls=%fused_computation.55 | convolution fusion | flops 1126105088 | bytes 19013632 | tf_op jit(solution)/shard_map/kgmn,nkd->mkgd/dot_general | solution.py:44
  269.5 1.5 copy.95
  271.0 1.0 broadcast_select_fusion.2
  272.2 5.6 %dynamic_update_slice.12 = bf16[1024,1024]{1,0:T(8,128)(2,1)S(1)} dynamic-update-slice(bf16[1024,1024]{1,0:T(8,128)(2,1)S(1)} %broadcast_in_dim.152, bf16[384,1024]{1,0:T(8,128)(2,1)} %broadcast_select_fusion.2, s32[]{:T(128)S(6)} %select_n.172, s32[]{:T(128)} %constant.145.clone.1) | dynamic-update-slice | bytes 1572868 | tf_op jit(solution)/shard_map/dynamic_update_slice | solution.py:110
  277.8 2.3 dynamic-slice_select_fusion.2
  280.2 5.5 %dynamic_update_slice.13 = bf16[1024,1024]{1,0:T(8,128)(2,1)S(1)} dynamic-update-slice(bf16[1024,1024]{1,0:T(8,128)(2,1)S(1)} %dynamic_update_slice.12, bf16[384,1024]{1,0:T(8,128)(2,1)} %dynamic-slice_select_fusion.2, s32[]{:T(128)S(6)} %select_n.182, s32[]{:T(128)} %constant.145.clone.1) | dynamic-update-slice | bytes 1572868 | tf_op jit(solution)/shard_map/dynamic_update_slice | solution.py:110
  285.7 2.3 dynamic-slice_select_fusion.1
  288.1 5.5 %dynamic_update_slice.14 = bf16[1024,1024]{1,0:T(8,128)(2,1)S(1)} dynamic-update-slice(bf16[1024,1024]{1,0:T(8,128)(2,1)S(1)} %dynamic_update_slice.13, bf16[384,1024]{1,0:T(8,128)(2,1)} %dynamic-slice_select_fusion.1, s32[]{:T(128)S(6)} %select_n.187, s32[]{:T(128)} %constant.145.clone.1) | dynamic-update-slice | bytes 1572868 | tf_op jit(solution)/shard_map/dynamic_update_slice | solution.py:110
  293.7 1.5 dynamic-slice_select_fusion
  295.2 4.7 %dynamic_update_slice.15 = bf16[1024,1024]{1,0:T(8,128)(2,1)} dynamic-update-slice(bf16[1024,1024]{1,0:T(8,128)(2,1)} %copy-done, bf16[384,1024]{1,0:T(8,128)(2,1)} %dynamic-slice_select_fusion, s32[]{:T(128)S(6)} %select_n.192, s32[]{:T(128)} %constant.145.clone.1) | dynamic-update-slice | bytes 1572868 | tf_op jit(solution)/shard_map/dynamic_update_slice | solution.py:110
  (101 shorter events, 15.0 us)
Async XLA Ops:
  29.5 9.8 %copy-start.3 = (bf16[2,128,1024]{2,1,0:T(8,128)(2,1)S(1)}, bf16[2,128,1024]{2,1,0:T(8,128)(2,1)}, u32[]{:S(2)}) copy-start(bf16[2,128,1024]{2,1,0:T(8,128)(2,1)} %param.8) | copy-start | bytes 1572868
  29.5 9.8 %copy-start.16 = (s32[1,4]{1,0:T(1,128)S(1)}, s32[1,4]{1,0:T(1,128)}, u32[]{:S(2)}) copy-start(s32[1,4]{1,0:T(1,128)} %param.13) | copy-start | bytes 52
  29.5 13.3 %copy-start.15 = (s32[4,8]{1,0:T(4,128)S(1)}, s32[4,8]{1,0:T(4,128)}, u32[]{:S(2)}) copy-start(s32[4,8]{1,0:T(4,128)} %param.10) | copy-start | bytes 388
  29.5 18.9 %copy-start.17 = (s32[4]{0:T(128)S(1)}, s32[4]{0:T(128)}, u32[]{:S(2)}) copy-start(s32[4]{0:T(128)} %param.12) | copy-start | bytes 52
  29.5 20.9 %copy-start.1 = (bf16[1024,1024]{1,0:T(8,128)(2,1)S(1)}, bf16[1024,1024]{1,0:T(8,128)(2,1)}, u32[]{:S(2)}) copy-start(bf16[1024,1024]{1,0:T(8,128)(2,1)} %param.7) | copy-start | bytes 6291460
  34.2 100.9 %all-to-all-start.1 = ((bf16[32,2,2,128,128]{4,3,2,1,0:T(8,128)(2,1)}), bf16[32,2,2,128,128]{4,3,2,1,0:T(8,128)(2,1)}, u32[]{:S(2)}, u32[]{:S(2)}) async-start(bf16[32,2,2,128,128]{4,3,2,1,0:T(8,128)(2,1)} %broadcast_select_fusion), calls=%async_computation.1 | async-start | bytes 8388608 | tf_op jit(solution)/shard_map/all_to_all | solution.py:65
  39.3 13.9 %collective-permute-start = (bf16[2,128,1024]{2,1,0:T(8,128)(2,1)S(1)}, bf16[2,128,1024]{2,1,0:T(8,128)(2,1)}, u32[]{:S(2)}, u32[]{:S(2)}) collective-permute-start(bf16[2,128,1024]{2,1,0:T(8,128)(2,1)S(1)} %copy-done.3), channel_id=1, source_target_pairs={{0,1},{1,2},{2,3},{3,4},{4,5},{5,6},{6,7},{7,0},{8,9},{9,10},{10,1... | collective-permute-start | bytes 1572872 | tf_op jit(solution)/shard_map/ppermute | solution.py:59
  53.2 8.8 %collective-permute-start.1 = (bf16[2,128,1024]{2,1,0:T(8,128)(2,1)}, bf16[2,128,1024]{2,1,0:T(8,128)(2,1)S(1)}, u32[]{:S(2)}, u32[]{:S(2)}) collective-permute-start(bf16[2,128,1024]{2,1,0:T(8,128)(2,1)} %collective-permute-done), channel_id=1, source_target_pairs={{0,1},{1,2},{2,3},{3,4},{4,5},{5,6},{6,7},{7,0},{8,9},{9,10},{10,1... | collective-permute-start | bytes 1572872 | tf_op jit(solution)/shard_map/ppermute | solution.py:59
  62.0 9.3 %copy-start.4 = (bf16[2,128,1024]{2,1,0:T(8,128)(2,1)}, bf16[2,128,1024]{2,1,0:T(8,128)(2,1)S(1)}, u32[]{:S(2)}) copy-start(bf16[2,128,1024]{2,1,0:T(8,128)(2,1)S(1)} %collective-permute-done.1) | copy-start | bytes 1572868
  62.0 8.6 %collective-permute-start.2 = (bf16[2,128,1024]{2,1,0:T(8,128)(2,1)S(1)}, bf16[2,128,1024]{2,1,0:T(8,128)(2,1)S(1)}, u32[]{:S(2)}, u32[]{:S(2)}) collective-permute-start(bf16[2,128,1024]{2,1,0:T(8,128)(2,1)S(1)} %collective-permute-done.1), channel_id=1, source_target_pairs={{0,1},{1,2},{2,3},{3,4},{4,5},{5,6},{6,7},{7,0},{8,9},{9,10},{10,1... | collective-permute-start | bytes 1572872 | tf_op jit(solution)/shard_map/ppermute | solution.py:59
  70.6 28.0 %copy-start.5 = (bf16[2,128,1024]{2,1,0:T(8,128)(2,1)}, bf16[2,128,1024]{2,1,0:T(8,128)(2,1)S(1)}, u32[]{:S(2)}) copy-start(bf16[2,128,1024]{2,1,0:T(8,128)(2,1)S(1)} %collective-permute-done.2) | copy-start | bytes 1572868
  70.6 8.6 %collective-permute-start.3 = (bf16[2,128,1024]{2,1,0:T(8,128)(2,1)S(1)}, bf16[2,128,1024]{2,1,0:T(8,128)(2,1)S(1)}, u32[]{:S(2)}, u32[]{:S(2)}) collective-permute-start(bf16[2,128,1024]{2,1,0:T(8,128)(2,1)S(1)} %collective-permute-done.2), channel_id=1, source_target_pairs={{0,1},{1,2},{2,3},{3,4},{4,5},{5,6},{6,7},{7,0},{8,9},{9,10},{10,1... | collective-permute-start | bytes 1572872 | tf_op jit(solution)/shard_map/ppermute | solution.py:59
  79.3 0.8 copy-start.7
  79.3 8.7 %collective-permute-start.4 = (bf16[2,128,1024]{2,1,0:T(8,128)(2,1)S(1)}, bf16[2,128,1024]{2,1,0:T(8,128)(2,1)}, u32[]{:S(2)}, u32[]{:S(2)}) collective-permute-start(bf16[2,128,1024]{2,1,0:T(8,128)(2,1)S(1)} %collective-permute-done.3), channel_id=1, source_target_pairs={{0,1},{1,2},{2,3},{3,4},{4,5},{5,6},{6,7},{7,0},{8,9},{9,10},{10,1... | collective-permute-start | bytes 1572872 | tf_op jit(solution)/shard_map/ppermute | solution.py:59
  88.0 9.1 %collective-permute-start.5 = (bf16[2,128,1024]{2,1,0:T(8,128)(2,1)}, bf16[2,128,1024]{2,1,0:T(8,128)(2,1)}, u32[]{:S(2)}, u32[]{:S(2)}) collective-permute-start(bf16[2,128,1024]{2,1,0:T(8,128)(2,1)} %collective-permute-done.4), channel_id=1, source_target_pairs={{0,1},{1,2},{2,3},{3,4},{4,5},{5,6},{6,7},{7,0},{8,9},{9,10},{10,1... | collective-permute-start | bytes 1572872 | tf_op jit(solution)/shard_map/ppermute | solution.py:59
  97.1 8.8 %collective-permute-start.6 = (bf16[2,128,1024]{2,1,0:T(8,128)(2,1)}, bf16[2,128,1024]{2,1,0:T(8,128)(2,1)S(1)}, u32[]{:S(2)}, u32[]{:S(2)}) collective-permute-start(bf16[2,128,1024]{2,1,0:T(8,128)(2,1)} %collective-permute-done.5), channel_id=1, source_target_pairs={{0,1},{1,2},{2,3},{3,4},{4,5},{5,6},{6,7},{7,0},{8,9},{9,10},{10,1... | collective-permute-start | bytes 1572872 | tf_op jit(solution)/shard_map/ppermute | solution.py:59
  98.7 17.1 %copy-start.6 = (bf16[2,128,1024]{2,1,0:T(8,128)(2,1)S(1)}, bf16[2,128,1024]{2,1,0:T(8,128)(2,1)}, u32[]{:S(2)}) copy-start(bf16[2,128,1024]{2,1,0:T(8,128)(2,1)} %copy-done.5) | copy-start | bytes 1572868
  188.7 9.5 %copy-start.14 = (bf16[384,1,128]{0,2,1:T(8,128)(2,1)S(1)}, bf16[384,1,128]{0,2,1:T(8,128)(2,1)}, u32[]{:S(2)}) copy-start(bf16[384,1,128]{0,2,1:T(8,128)(2,1)} %copy.103) | copy-start | bytes 294916
  198.1 13.1 %copy-start.9 = (bf16[1,8,1,128,128]{4,3,2,1,0:T(8,128)(2,1)S(1)}, bf16[1,8,1,128,128]{4,3,2,1,0:T(8,128)(2,1)}, u32[]{:S(2)}) copy-start(bf16[1,8,1,128,128]{4,3,2,1,0:T(8,128)(2,1)} %get-tuple-element.18) | copy-start | bytes 786436
  198.1 14.0 %copy-start.11 = (bf16[384,1,128]{2,0,1:T(8,128)(2,1)S(1)}, bf16[384,1,128]{2,0,1:T(8,128)(2,1)}, u32[]{:S(2)}) copy-start(bf16[384,1,128]{2,0,1:T(8,128)(2,1)} %get-tuple-element.11) | copy-start | bytes 294916
  221.0 9.5 %copy-start.13 = (bf16[384,1,128]{0,2,1:T(8,128)(2,1)S(1)}, bf16[384,1,128]{0,2,1:T(8,128)(2,1)}, u32[]{:S(2)}) copy-start(bf16[384,1,128]{0,2,1:T(8,128)(2,1)} %copy.97) | copy-start | bytes 294916
  230.5 11.0 %copy-start.8 = (bf16[1,8,1,128,128]{4,3,2,1,0:T(8,128)(2,1)S(1)}, bf16[1,8,1,128,128]{4,3,2,1,0:T(8,128)(2,1)}, u32[]{:S(2)}) copy-start(bf16[1,8,1,128,128]{4,3,2,1,0:T(8,128)(2,1)} %get-tuple-element.20) | copy-start | bytes 786436
  230.5 11.1 %copy-start.10 = (bf16[384,1,128]{2,0,1:T(8,128)(2,1)S(1)}, bf16[384,1,128]{2,0,1:T(8,128)(2,1)}, u32[]{:S(2)}) copy-start(bf16[384,1,128]{2,0,1:T(8,128)(2,1)} %get-tuple-element.12) | copy-start | bytes 294916
  249.5 9.5 %copy-start.12 = (bf16[384,1,128]{0,2,1:T(8,128)(2,1)S(1)}, bf16[384,1,128]{0,2,1:T(8,128)(2,1)}, u32[]{:S(2)}) copy-start(bf16[384,1,128]{0,2,1:T(8,128)(2,1)} %copy.91) | copy-start | bytes 294916
  269.5 24.2 %copy-start.2 = (bf16[384,1024]{1,0:T(8,128)(2,1)S(1)}, bf16[384,1024]{1,0:T(8,128)(2,1)}, u32[]{:S(2)}) copy-start(bf16[384,1024]{1,0:T(8,128)(2,1)} %copy.113) | copy-start | bytes 2359300
  293.6 1.6 copy-start
